TPU v7x, 32 devices: a whole 2x2x4 slice. The times are simulated.
32 devices in a mesh: rep: 2 (over x), zero: 16 (over z, y, core).
Axes of the slice: x: 2, y: 2, z: 4, core: 2. Of those that a mesh axis runs over, the one named last changes fastest.
Arguments:
- gated_input: bfloat16 [2, 2048, 4096], P('rep', 'zero'), may hold values from -6 to 6
- query_gate: bfloat16 [2, 2048, 4096], P('rep', 'zero'), may hold values from -12 to 12
- cotangent: bfloat16 [2, 2048, 4096], P('rep', 'zero'), may hold values from -8 to 8
- filters: float32 [2, 256, 128], P('rep', 'zero'), may hold values from -0.5 to 0.5
- first_moment: float32 [2, 256, 128], P('rep', 'zero'), may hold values from -0.03125 to 0.03125
- second_moment: float32 [2, 256, 128], P('rep', 'zero'), may hold values from 1e-06 to 0.0001
- step_index: int32 [1], replicated, may hold values from 0 to 999
Outputs:
- query_grad: bfloat16 [2, 2048, 4096], P('rep', 'zero')
- input_grad: bfloat16 [2, 2048, 4096], P('rep', 'zero')
- new_filters: float32 [2, 256, 128], P('rep', 'zero')
All inputs are finite; a program needn't handle non-finite values.
Results may differ from a plain program's by a relative error of at most 0.007.
Values may be sent and summed in bfloat16 or wider, within the bound.
No kernel may reach another device: no remote copies, remote signals or barrier semaphores. Data moves between devices by JAX's collectives and lax.ppermute only.
A program may use at most 256 MiB of HBM per device.

v0:
```python
from functools import partial
import jax
import jax.numpy as jnp
from jax import lax
from jax.sharding import PartitionSpec as P

CLIP_NORM = 1.0
BETA_ONE = 0.9
BETA_TWO = 0.95
LEARN_RATE = 0.05
ADAM_EPS = 1e-08


def swapped(value, axis, apart):
    mask = 2**apart
    pairs = [(source, source ^ mask) for source in range(lax.axis_size(axis))]
    return lax.ppermute(value, axis, pairs)


def passed_along(block, axis, distance):
    devices = range(lax.axis_size(axis))
    route = [(i - distance, i) for i in devices if i - distance in devices]
    return lax.ppermute(block, axis, route)


def circulant(half_filters):
    groups_all, filter_len = half_filters.shape
    flipped = half_filters[:, ::-1]
    doubled = jnp.concatenate([flipped, flipped], axis=1)
    tiled = jnp.tile(doubled, (1, filter_len))
    trimmed = tiled[:, : filter_len * (2 * filter_len - 1)]
    return trimmed.reshape(groups_all, filter_len, 2 * filter_len - 1)[:, :, filter_len - 1 :]


def blocked(rows_major, groups_all, filter_len):
    tok_rows, channels = rows_major.shape
    return rows_major.T.reshape(
        groups_all, channels // groups_all, tok_rows // filter_len, filter_len
    )


def unblocked(blocks):
    groups_all, group_width, block_count, filter_len = blocks.shape
    return blocks.reshape(groups_all * group_width, block_count * filter_len).T


def swap_bit(values, bit_number):
    return swapped(values, "rep", bit_number)


def on_device(gated_input, query_gate, cotangent, filters, first_moment, second_moment, step_index):
    inputs = gated_input[0]
    gate_values = query_gate[0]
    upstream = cotangent[0]
    tok_rows, channels = inputs.shape
    filter_len = filters.shape[2]
    shard_len = filters.shape[1]
    half_filters = lax.all_gather(filters[0].astype(jnp.bfloat16), "zero", axis=0, tiled=True)
    groups_all = half_filters.shape[0]
    circ_table = circulant(half_filters)
    index_row = lax.broadcasted_iota(jnp.int32, (filter_len, filter_len), 0)
    index_col = lax.broadcasted_iota(jnp.int32, (filter_len, filter_len), 1)
    lower_mask = (index_row >= index_col)[None]
    zero_half = jnp.zeros((), jnp.bfloat16)
    table_cur = jnp.where(lower_mask, circ_table, zero_half)
    table_prev = jnp.where(lower_mask, zero_half, circ_table)
    upstream_wide = upstream.astype(jnp.float32)
    mixed_rows = (upstream_wide * gate_values.astype(jnp.float32)).astype(jnp.bfloat16)
    tail_rows = passed_along(inputs, "zero", 1)
    head_rows = passed_along(mixed_rows, "zero", -1)
    input_ext = jnp.concatenate([tail_rows, inputs], axis=0)
    mixed_ext = jnp.concatenate([mixed_rows, head_rows], axis=0)
    input_blocks = blocked(input_ext, groups_all, filter_len)
    mixed_blocks = blocked(mixed_ext, groups_all, filter_len)
    input_cur = input_blocks[:, :, 1:]
    input_prev = input_blocks[:, :, :-1]
    mixed_own = mixed_blocks[:, :, :-1]
    mixed_next = mixed_blocks[:, :, 1:]
    conv_out = jnp.einsum(
        "gik,gcbk->gcbi", table_cur, input_cur, preferred_element_type=jnp.float32
    )
    conv_out = conv_out + jnp.einsum(
        "gik,gcbk->gcbi", table_prev, input_prev, preferred_element_type=jnp.float32
    )
    query_grad = (upstream_wide * unblocked(conv_out)).astype(jnp.bfloat16)
    back_blocks = jnp.einsum(
        "gki,gcbk->gcbi", table_cur, mixed_own, preferred_element_type=jnp.float32
    )
    back_blocks = back_blocks + jnp.einsum(
        "gki,gcbk->gcbi", table_prev, mixed_next, preferred_element_type=jnp.float32
    )
    input_grad = unblocked(back_blocks).astype(jnp.bfloat16)
    lag_cur = jnp.einsum("gcbi,gcbk->gik", mixed_own, input_cur, preferred_element_type=jnp.float32)
    lag_prev = jnp.einsum(
        "gcbi,gcbk->gik", mixed_own, input_prev, preferred_element_type=jnp.float32
    )
    square = filter_len * filter_len
    front_part = jnp.pad(
        jnp.where(lower_mask, lag_cur, 0.0).reshape(groups_all, square), ((0, 0), (filter_len, 0))
    )
    rear_part = jnp.pad(
        jnp.where(lower_mask, 0.0, lag_prev).reshape(groups_all, square), ((0, 0), (0, filter_len))
    )
    skewed = (front_part + rear_part).reshape(groups_all, filter_len, filter_len + 1).sum(axis=1)
    local_grad = skewed[:, 1:][:, ::-1]
    grad_full = lax.psum(local_grad.astype(jnp.bfloat16), "zero").astype(jnp.float32)
    total_sq = jnp.sum(grad_full * grad_full)
    grad_shard = lax.dynamic_slice_in_dim(
        grad_full, lax.axis_index("zero") * shard_len, shard_len, 0
    )
    clip_scale = jnp.minimum(1.0, CLIP_NORM / (jnp.sqrt(total_sq) + 1e-06))
    clipped = grad_shard * clip_scale
    step_count = step_index[0].astype(jnp.float32) + 1.0
    moment_one = BETA_ONE * first_moment[0] + (1.0 - BETA_ONE) * clipped
    moment_two = BETA_TWO * second_moment[0] + (1.0 - BETA_TWO) * clipped * clipped
    corrected_one = moment_one / (1.0 - jnp.power(BETA_ONE, step_count))
    corrected_two = moment_two / (1.0 - jnp.power(BETA_TWO, step_count))
    stepped = filters[0] - LEARN_RATE * corrected_one / (jnp.sqrt(corrected_two) + ADAM_EPS)
    bit_count = lax.axis_size("rep").bit_length() - 1
    partner_bit = step_index[0] % bit_count
    branches = [partial(swap_bit, bit_number=number) for number in range(bit_count)]
    partner_values = lax.switch(partner_bit, branches, stepped)
    new_filters = 0.5 * (stepped + partner_values)
    return (query_grad[None], input_grad[None], new_filters[None])


def solution(mesh):
    return jax.shard_map(
        on_device,
        mesh=mesh,
        in_specs=(
            P("rep", "zero", None),
            P("rep", "zero", None),
            P("rep", "zero", None),
            P("rep", "zero", None),
            P("rep", "zero", None),
            P("rep", "zero", None),
            P(),
        ),
        out_specs=(P("rep", "zero", None), P("rep", "zero", None), P("rep", "zero", None)),
        check_vma=False,
    )
```

profile of v0, /device:TPU:8, one launch (start us, length us, event | category | flops | bytes accessed | tf_op | source)
XLA Modules:
  0.0 408.8 jit_solution(13536019468429333070)
XLA Ops:
  7.2 1.9 collective-permute-start
  9.8 23.5 %all_gather.3 = bf16[256,128]{1,0:T(8,128)(2,1)S(1)} all-gather(bf16[16,128]{1,0:T(8,128)(2,1)S(1)} %bitcast_convert_fusion), channel_id=1, replica_groups=mesh['rep'=2,'zero'=16] {'zero'}, dimensions={0}, use_global_device_ids=true | all-gather | bytes 69632 | tf_op jit(solution)/shard_map/all_gather | solution.py:58
  34.8 41.7 %copy.70 = bf16[32,8,128,256]{3,1,2,0:T(8,128)(2,1)S(1)} copy(bf16[32,8,128,256]{3,2,1,0:T(8,128)(2,1)S(1)} %bitcast.64) | data formatting | bytes 33554432
  76.5 6.6 %slice.29 = bf16[256,32640]{1,0:T(8,128)(2,1)} slice(bf16[256,32768]{1,0:T(8,128)(2,1)S(1)} %bitcast.65), slice={[0:256], [0:32640]} | slice | bytes 33423360 | tf_op jit(solution)/shard_map/slice | solution.py:31
  83.1 56.8 %reshape.85 = bf16[256,128,255]{2,1,0:T(8,128)(2,1)} reshape(bf16[256,32640]{1,0:T(8,128)(2,1)} %slice.29) | data formatting | bytes 33423360 | tf_op jit(solution)/shard_map/reshape | solution.py:32
  140.0 1.4 maximum_bitcast_fusion
  141.4 2.5 copy.52
  143.9 2.5 reshape.83
  146.4 3.0 fusion.25
  149.4 9.6 %fusion.1 = f32[256,16,128]{2,1,0:T(8,128)S(1)} fusion(pred[128,128]{1,0:T(8,128)(4,1)S(1)} %iota_compare_fusion, bf16[256,128,255]{2,1,0:T(8,128)(2,1)} %reshape.85, bf16[256,16,1,128]{3,2,1,0:T(2,128)(2,1)S(1)} %get-tuple-element.12), kind=kOutput, calls=%fused_computation.6 | convolution fusion | flops 138412032 | bytes 11550720 | tf_op jit(solution)/shard_map/gik,gcbk->gcbi/dot_general | solution.py:79
  159.1 11.7 %fusion.10 = f32[256,16,128]{2,1,0:T(8,128)} fusion(f32[256,16,128]{2,1,0:T(8,128)S(1)} %fusion.1, pred[128,128]{1,0:T(8,128)(4,1)S(1)} %iota_compare_fusion, bf16[256,128,255]{2,1,0:T(8,128)(2,1)} %reshape.85, bf16[256,16,1,128]{3,2,1,0:T(2,128)(2,1)S(1)} %get-tuple-element.11), kind=kOutput, calls=%fused_computation.20 | convolution fusion | flops 138936320 | bytes 13647872 | tf_op jit(solution)/shard_map/gik,gcbk->gcbi/dot_general | solution.py:82
  170.8 2.1 copy.55
  172.9 3.0 fusion.9
  175.9 3.7 collective-permute-start.1
  180.3 11.6 %collective-permute-done.1 = bf16[128,4096]{1,0:T(8,128)(2,1)} collective-permute-done((bf16[128,4096]{1,0:T(8,128)(2,1)S(1)}, bf16[128,4096]{1,0:T(8,128)(2,1)}, u32[]{:S(2)}, u32[]{:S(2)}) %collective-permute-start.1) | collective-permute-done | bytes 1048608 | tf_op jit(solution)/shard_map/ppermute | solution.py:23
  191.9 1.4 maximum_bitcast_fusion.1
  193.3 2.5 copy.56
  195.8 2.5 reshape.88
  198.3 3.8 fusion.24
  202.1 7.2 %convolution_select_fusion = f32[256,128,128]{2,1,0:T(8,128)} fusion(pred[128,128]{1,0:T(8,128)(4,1)S(1)} %iota_compare_fusion, bf16[256,16,1,128]{3,2,1,0:T(2,128)(2,1)S(1)} %copy-done.5, bf16[256,16,1,128]{3,2,1,0:T(2,128)(2,1)S(1)} %get-tuple-element.10), kind=kOutput, calls=%fused_computation.1 | convolution fusion | flops 138412032 | bytes 18890752 | tf_op jit(solution)/shard_map/gcbi,gcbk->gik/dot_general | solution.py:94
  209.3 7.1 %convolution_select_fusion.1 = f32[256,128,128]{2,1,0:T(8,128)} fusion(pred[128,128]{1,0:T(8,128)(4,1)S(1)} %iota_compare_fusion, bf16[256,16,1,128]{3,2,1,0:T(2,128)(2,1)S(1)} %copy-done.3, bf16[256,16,1,128]{3,2,1,0:T(2,128)(2,1)S(1)} %get-tuple-element.10), kind=kOutput, calls=%fused_computation.2 | convolution fusion | flops 138412032 | bytes 18890752 | tf_op jit(solution)/shard_map/gcbi,gcbk->gik/dot_general | solution.py:93
  216.4 17.7 %copy.64 = f32[256,128,128]{0,2,1:T(8,128)} copy(f32[256,128,128]{2,1,0:T(8,128)} %convolution_select_fusion) | data formatting | bytes 33554432 | tf_op jit(solution)/shard_map/reshape | solution.py:102
  234.1 17.7 %copy.63 = f32[256,128,128]{0,2,1:T(8,128)} copy(f32[256,128,128]{2,1,0:T(8,128)} %convolution_select_fusion.1) | data formatting | bytes 33554432 | tf_op jit(solution)/shard_map/reshape | solution.py:99
  251.9 18.0 %pad_add_fusion = f32[256,16512]{0,1:T(8,128)} fusion(f32[256,16384]{0,1:T(8,128)} %bitcast.62, f32[256,16384]{0,1:T(8,128)} %bitcast.63), kind=kLoop, calls=%fused_computation | loop fusion | flops 4227072 | bytes 50462720 | tf_op jit(solution)/shard_map/add | solution.py:104
  269.9 18.0 %reshape.93 = f32[256,128,129]{0,2,1:T(8,128)} reshape(f32[256,16512]{0,1:T(8,128)} %pad_add_fusion) | data formatting | bytes 33816576 | tf_op jit(solution)/shard_map/reshape | solution.py:104
  287.9 7.3 %reduce_sum.18 = bf16[256,129]{0,1:T(8,128)(2,1)S(1)} reduce(f32[256,128,129]{0,2,1:T(8,128)} %reshape.93, f32[]{:T(128)} %constant.9.clone.1), dimensions={1}, to_apply=%region_0.1 | reduce | flops 4194048 | bytes 16974340 | tf_op jit(solution)/shard_map/reduce_sum | solution.py:104
  296.2 10.4 %fusion = f32[256,16,128]{2,1,0:T(8,128)} fusion(pred[128,128]{1,0:T(8,128)(4,1)S(1)} %iota_compare_fusion, bf16[256,128,255]{2,1,0:T(8,128)(2,1)} %reshape.85, bf16[256,16,1,128]{3,2,1,0:T(2,128)(2,1)S(1)} %copy-done.1), kind=kOutput, calls=%fused_computation.5 | convolution fusion | flops 138412032 | bytes 11550720 | tf_op jit(solution)/shard_map/gki,gcbk->gcbi/dot_general | solution.py:86
  306.5 78.4 %all-reduce.4.cloned.1.call-done = bf16[256,128]{1,0:T(8,128)(2,1)} async-done(((bf16[256,128]{1,0:T(8,128)(2,1)}), bf16[256,128]{1,0:T(8,128)(2,1)}) %all-reduce.4.cloned.1.call-update) | async-done | bytes 65552 | tf_op jit(solution)/shard_map/psum | solution.py:106
  385.0 1.5 multiply_reduce_fusion
  388.1 1.5 collective-permute-start.2
  389.6 10.4 %add_convert_fusion = bf16[256,16,128]{2,1,0:T(8,128)(2,1)S(1)} fusion(f32[256,16,128]{2,1,0:T(8,128)} %fusion, pred[128,128]{1,0:T(8,128)(4,1)S(1)} %iota_compare_fusion, bf16[256,128,255]{2,1,0:T(8,128)(2,1)} %reshape.85, bf16[256,16,1,128]{3,2,1,0:T(2,128)(2,1)} %get-tuple-element.9), kind=kOutput, calls=%fused_computation.19 | convolution fusion | flops 139460608 | bytes 13647872 | tf_op jit(solution)/shard_map/gki,gcbk->gcbi/dot_general | solution.py:89
  400.0 1.3 copy.59
  (35 shorter events, 4.7 us)
Async XLA Ops:
  7.2 377.8 %all-reduce.4.cloned.1.call-start = ((), (), s32[]{:S(2)}) async-start(), calls=%async_computation | async-start | bytes 131072 | tf_op jit(solution)/shard_map/psum | solution.py:106
  7.2 132.8 %collective-permute-start = (bf16[128,4096]{1,0:T(8,128)(2,1)}, bf16[128,4096]{1,0:T(8,128)(2,1)}, u32[]{:S(2)}, u32[]{:S(2)}) collective-permute-start(bf16[128,4096]{1,0:T(8,128)(2,1)} %bitcast.69), channel_id=1, source_target_pairs={{0,1},{1,2},{2,3},{3,4},{4,5},{5,6},{6,7},{7,8},{8,9},{9,10},{10,1... | collective-permute-start | bytes 3145736 | tf_op jit(solution)/shard_map/ppermute | solution.py:23
  83.1 56.8 %copy-start.6 = (bf16[1,128,4096]{2,1,0:T(8,128)(2,1)S(1)}, bf16[1,128,4096]{2,1,0:T(8,128)(2,1)}, u32[]{:S(2)}) copy-start(bf16[1,128,4096]{2,1,0:T(8,128)(2,1)} %param.7) | copy-start | bytes 3145732
  149.4 9.7 %copy-start.2 = (bf16[256,16,1,128]{3,2,1,0:T(2,128)(2,1)}, bf16[256,16,1,128]{3,2,1,0:T(2,128)(2,1)S(1)}, u32[]{:S(2)}) copy-start(bf16[256,16,1,128]{3,2,1,0:T(2,128)(2,1)S(1)} %get-tuple-element.12) | copy-start | bytes 3145732
  149.4 9.7 %copy-start.4 = (bf16[256,16,1,128]{3,2,1,0:T(2,128)(2,1)}, bf16[256,16,1,128]{3,2,1,0:T(2,128)(2,1)S(1)}, u32[]{:S(2)}) copy-start(bf16[256,16,1,128]{3,2,1,0:T(2,128)(2,1)S(1)} %get-tuple-element.11) | copy-start | bytes 3145732
  175.9 16.0 %collective-permute-start.1 = (bf16[128,4096]{1,0:T(8,128)(2,1)S(1)}, bf16[128,4096]{1,0:T(8,128)(2,1)}, u32[]{:S(2)}, u32[]{:S(2)}) collective-permute-start(bf16[128,4096]{1,0:T(8,128)(2,1)S(1)} %get-tuple-element.13), channel_id=1, source_target_pairs={{1,0},{2,1},{3,2},{4,3},{5,4},{6,5},{7,6},{8,7},{9,8},{10,9},{11,1... | collective-permute-start | bytes 3145736 | tf_op jit(solution)/shard_map/ppermute | solution.py:23
  198.3 3.8 copy-start.5
  202.1 7.2 %copy-start = (bf16[256,16,1,128]{3,2,1,0:T(2,128)(2,1)}, bf16[256,16,1,128]{3,2,1,0:T(2,128)(2,1)S(1)}, u32[]{:S(2)}) copy-start(bf16[256,16,1,128]{3,2,1,0:T(2,128)(2,1)S(1)} %get-tuple-element.10) | copy-start | bytes 3145732
  202.1 7.2 %copy-start.3 = (bf16[256,16,1,128]{3,2,1,0:T(2,128)(2,1)S(1)}, bf16[256,16,1,128]{3,2,1,0:T(2,128)(2,1)}, u32[]{:S(2)}) copy-start(bf16[256,16,1,128]{3,2,1,0:T(2,128)(2,1)} %copy-done.2) | copy-start | bytes 3145732
  287.9 8.3 %copy-start.1 = (bf16[256,16,1,128]{3,2,1,0:T(2,128)(2,1)S(1)}, bf16[256,16,1,128]{3,2,1,0:T(2,128)(2,1)}, u32[]{:S(2)}) copy-start(bf16[256,16,1,128]{3,2,1,0:T(2,128)(2,1)} %copy-done) | copy-start | bytes 3145732
  296.1 91.9 %copy-start.7 = (f32[1,16,128]{2,1,0:T(8,128)S(1)}, f32[1,16,128]{2,1,0:T(8,128)}, u32[]{:S(2)}) copy-start(f32[1,16,128]{2,1,0:T(8,128)} %param.10) | copy-start | bytes 24580
  296.2 91.9 %copy-start.8 = (f32[1,16,128]{2,1,0:T(8,128)S(1)}, f32[1,16,128]{2,1,0:T(8,128)}, u32[]{:S(2)}) copy-start(f32[1,16,128]{2,1,0:T(8,128)} %param.12) | copy-start | bytes 24580
  296.2 91.9 %copy-start.9 = (f32[1,16,128]{2,1,0:T(8,128)S(1)}, f32[1,16,128]{2,1,0:T(8,128)}, u32[]{:S(2)}) copy-start(f32[1,16,128]{2,1,0:T(8,128)} %param.11) | copy-start | bytes 24580
  388.1 13.2 %collective-permute-start.2 = (f32[16,128]{1,0:T(8,128)S(1)}, f32[16,128]{1,0:T(8,128)S(1)}, u32[]{:S(2)}, u32[]{:S(2)}) collective-permute-start(f32[16,128]{1,0:T(8,128)S(1)} %fusion.17), channel_id=1, source_target_pairs={{0,16},{16,0},{1,17},{17,1},{2,18},{18,2},{3,19},{19,3},{4,20},{20... | collective-permute-start | bytes 24584 | tf_op jit(solution)/shard_map/ppermute | solution.py:17
Sparse Core Ops, SparseCore 0:
  296.3 88.6 all-reduce.3
where the time goes:
time: 410 us; the launch traced here: 409 us
  local copies, waits for them, and re-layouts  181 us (44%)
  waiting for transfers between devices  90 us (22%)
  matrix products  56.3 us (14%)
  other arithmetic  34.8 us (8%)
  blocking collectives  23.5 us (6%)
  between operations  15.7 us (4%)
  starting transfers between devices  7.19 us (2%)
    psum x1, waiting for transfers between devices, on_device(): lax.psum(local_grad.astype(jnp.bfloat16), 'zero').astype(jnp.float32)  78.4 us
    reshape x1, local copies, waits for them, and re-layouts, circulant(): trimmed.reshape(groups_all, filter_len, 2 * filter_len - 1)  56.8 us
    unnamed x22, local copies, waits for them, and re-layouts  41.9 us
    all_gather x1, blocking collectives, on_device(): lax.all_gather(filters[0].astype(jnp.bfloat16), 'zero', axis=0, tiled=True)  23.5 us
    add x1, other arithmetic, on_device(): front_part + rear_part  18 us
    reshape x1, local copies, waits for them, and re-layouts, on_device(): (front_part + rear_part).reshape(groups_all, filter_len, filter_len + 1)  18 us
    reshape x1, local copies, waits for them, and re-layouts, on_device(): jnp.where(lower_mask, 0.0, lag_prev).reshape(groups_all, square)  17.7 us
    reshape x1, local copies, waits for them, and re-layouts, on_device(): jnp.where(lower_mask, lag_cur, 0.0).reshape(groups_all, square)  17.7 us
  transfers between devices with their start and end apart: 4, of which 2 were waited for; matrix products, arithmetic and copies ran while one was open for 32% of the time, Pallas kernels for 0%

commit v1 on v0

--- a/solution.py
+++ b/solution.py
@@ -55,7 +55,26 @@
     tok_rows, channels = inputs.shape
     filter_len = filters.shape[2]
     shard_len = filters.shape[1]
-    half_filters = lax.all_gather(filters[0].astype(jnp.bfloat16), "zero", axis=0, tiled=True)
+    value_2 = filters[0].astype(jnp.bfloat16)
+    size, mine, width = (lax.axis_size("zero"), lax.axis_index("zero"), value_2.shape[0])
+    right = [(i_2, (i_2 + 1) % size) for i_2 in range(size)]
+    left = [(i_2, (i_2 - 1) % size) for i_2 in range(size)]
+    half_filters = jnp.zeros(
+        (*value_2.shape[:0], size * width, *value_2.shape[0 + 1 :]), value_2.dtype
+    )
+    half_filters = lax.dynamic_update_slice_in_dim(half_filters, value_2, mine * width, axis=0)
+    from_left = from_right = value_2
+    half = size // 2
+    for step in range(1, half + 1):
+        from_left = lax.ppermute(from_left, "zero", right)
+        half_filters = lax.dynamic_update_slice_in_dim(
+            half_filters, from_left, (mine - step) % size * width, axis=0
+        )
+        if step < size - half:
+            from_right = lax.ppermute(from_right, "zero", left)
+            half_filters = lax.dynamic_update_slice_in_dim(
+                half_filters, from_right, (mine + step) % size * width, axis=0
+            )
     groups_all = half_filters.shape[0]
     circ_table = circulant(half_filters)
     index_row = lax.broadcasted_iota(jnp.int32, (filter_len, filter_len), 0)

time: 410 us -> 427 us (1.041)
  waiting for transfers between devices: 90 us -> 114 us
  blocking collectives: 23.5 us -> 0 us
  starting transfers between devices: 7.19 us -> 23.9 us
    all_gather x1 -> x0, blocking collectives: 23.5 us -> none  [on_device(): lax.all_gather(filters[0].astype(jnp.bfloat16), 'zero', axis=0, tiled=True)]
    ppermute x0 -> x15, waiting for transfers between devices: none -> 22.8 us  [the longest x8 22.6 us: on_device(): from_left = lax.ppermute(from_left, 'zero', right)]
    ppermute x0 -> x15, starting transfers between devices: none -> 18.5 us  [the longest x7 17.7 us: on_device(): from_right = lax.ppermute(from_right, 'zero', left)]
    unnamed x22 -> x24, local copies, waits for them, and re-layouts: 41.9 us -> 41.9 us
  transfers between devices with their start and end apart: 4 -> 19, of which waited for: 2 -> 9; matrix products, arithmetic and copies ran while one was open for 32% -> 30% of each run, Pallas kernels for 0% -> 0%
where the time goes in v1:
time: 427 us; the launch traced here: 425 us
  local copies, waits for them, and re-layouts  182 us (43%)
  waiting for transfers between devices  114 us (27%)
  matrix products  56.2 us (13%)
  other arithmetic  33.1 us (8%)
  starting transfers between devices  23.9 us (6%)
  between operations  16 us (4%)
    psum x1, waiting for transfers between devices, on_device(): lax.psum(local_grad.astype(jnp.bfloat16), 'zero').astype(jnp.float32)  80 us
    reshape x1, local copies, waits for them, and re-layouts, circulant(): trimmed.reshape(groups_all, filter_len, 2 * filter_len - 1)  56.8 us
    unnamed x24, local copies, waits for them, and re-layouts  41.9 us
    ppermute x8, waiting for transfers between devices, on_device(): from_left = lax.ppermute(from_left, 'zero', right)  22.6 us
    reshape x1, local copies, waits for them, and re-layouts, on_device(): (front_part + rear_part).reshape(groups_all, filter_len, filter_len + 1)  18 us
    add x1, other arithmetic, on_device(): front_part + rear_part  18 us
    reshape x1, local copies, waits for them, and re-layouts, on_device(): jnp.where(lower_mask, 0.0, lag_prev).reshape(groups_all, square)  17.8 us
    reshape x1, local copies, waits for them, and re-layouts, on_device(): jnp.where(lower_mask, lag_cur, 0.0).reshape(groups_all, square)  17.8 us
  transfers between devices with their start and end apart: 19, of which 9 were waited for; matrix products, arithmetic and copies ran while one was open for 30% of the time, Pallas kernels for 0%

profile of v1, /device:TPU:8, one launch (start us, length us, event | category | flops | bytes accessed | tf_op | source)
XLA Modules:
  0.0 425.4 jit_solution(3636167298958555643)
XLA Ops:
  7.9 2.6 collective-permute-start.2
  15.6 12.4 %collective-permute-done.3 = bf16[16,128]{1,0:T(8,128)(2,1)S(1)} collective-permute-done((bf16[16,128]{1,0:T(8,128)(2,1)S(1)}, bf16[16,128]{1,0:T(8,128)(2,1)S(1)}, u32[]{:S(2)}, u32[]{:S(2)}) %collective-permute-start.3) | collective-permute-done | bytes 4128 | tf_op jit(solution)/shard_map/ppermute | solution.py:69
  28.0 2.6 collective-permute-start.6
  31.9 2.6 collective-permute-start.8
  35.9 2.6 collective-permute-start.10
  39.8 2.6 collective-permute-start.12
  43.7 2.6 collective-permute-start.14
  47.7 3.9 collective-permute-done.15
  53.1 41.7 %copy.70 = bf16[32,8,128,256]{3,1,2,0:T(8,128)(2,1)S(1)} copy(bf16[32,8,128,256]{3,2,1,0:T(8,128)(2,1)S(1)} %bitcast.65) | data formatting | bytes 33554432
  94.8 6.8 %slice.29 = bf16[256,32640]{1,0:T(8,128)(2,1)} slice(bf16[256,32768]{1,0:T(8,128)(2,1)S(1)} %bitcast.66), slice={[0:256], [0:32640]} | slice | bytes 33423360 | tf_op jit(solution)/shard_map/slice | solution.py:31
  101.5 56.8 %reshape.85 = bf16[256,128,255]{2,1,0:T(8,128)(2,1)} reshape(bf16[256,32640]{1,0:T(8,128)(2,1)} %slice.29) | data formatting | bytes 33423360 | tf_op jit(solution)/shard_map/reshape | solution.py:32
  159.8 2.5 copy.52
  162.2 2.5 reshape.83
  164.8 3.0 fusion.25
  167.8 9.6 %fusion.1 = f32[256,16,128]{2,1,0:T(8,128)S(1)} fusion(pred[128,128]{1,0:T(8,128)(4,1)S(1)} %iota_compare_fusion, bf16[256,128,255]{2,1,0:T(8,128)(2,1)} %reshape.85, bf16[256,16,1,128]{3,2,1,0:T(2,128)(2,1)S(1)} %get-tuple-element.11), kind=kOutput, calls=%fused_computation.6 | convolution fusion | flops 138412032 | bytes 11550720 | tf_op jit(solution)/shard_map/gik,gcbk->gcbi/dot_general | solution.py:98
  177.4 11.7 %fusion.10 = f32[256,16,128]{2,1,0:T(8,128)} fusion(f32[256,16,128]{2,1,0:T(8,128)S(1)} %fusion.1, pred[128,128]{1,0:T(8,128)(4,1)S(1)} %iota_compare_fusion, bf16[256,128,255]{2,1,0:T(8,128)(2,1)} %reshape.85, bf16[256,16,1,128]{3,2,1,0:T(2,128)(2,1)S(1)} %get-tuple-element.10), kind=kOutput, calls=%fused_computation.20 | convolution fusion | flops 138936320 | bytes 13647872 | tf_op jit(solution)/shard_map/gik,gcbk->gcbi/dot_general | solution.py:101
  189.1 2.2 copy.55
  191.3 2.6 fusion.9
  196.6 11.6 %collective-permute-done.16 = bf16[128,4096]{1,0:T(8,128)(2,1)S(1)} collective-permute-done((bf16[128,4096]{1,0:T(8,128)(2,1)S(1)}, bf16[128,4096]{1,0:T(8,128)(2,1)S(1)}, u32[]{:S(2)}, u32[]{:S(2)}) %collective-permute-start.16) | collective-permute-done | bytes 1048608 | tf_op jit(solution)/shard_map/ppermute | solution.py:23
  208.3 2.5 copy.56
  210.7 2.5 reshape.88
  213.3 3.8 fusion.24
  217.1 7.2 %convolution_select_fusion = f32[256,128,128]{2,1,0:T(8,128)} fusion(pred[128,128]{1,0:T(8,128)(4,1)S(1)} %iota_compare_fusion, bf16[256,16,1,128]{3,2,1,0:T(2,128)(2,1)S(1)} %copy-done.5, bf16[256,16,1,128]{3,2,1,0:T(2,128)(2,1)S(1)} %get-tuple-element.9), kind=kOutput, calls=%fused_computation.1 | convolution fusion | flops 138412032 | bytes 18890752 | tf_op jit(solution)/shard_map/gcbi,gcbk->gik/dot_general | solution.py:113
  224.3 7.1 %convolution_select_fusion.1 = f32[256,128,128]{2,1,0:T(8,128)} fusion(pred[128,128]{1,0:T(8,128)(4,1)S(1)} %iota_compare_fusion, bf16[256,16,1,128]{3,2,1,0:T(2,128)(2,1)S(1)} %copy-done.3, bf16[256,16,1,128]{3,2,1,0:T(2,128)(2,1)S(1)} %get-tuple-element.9), kind=kOutput, calls=%fused_computation.2 | convolution fusion | flops 138412032 | bytes 18890752 | tf_op jit(solution)/shard_map/gcbi,gcbk->gik/dot_general | solution.py:112
  231.4 17.8 %copy.64 = f32[256,128,128]{0,2,1:T(8,128)} copy(f32[256,128,128]{2,1,0:T(8,128)} %convolution_select_fusion) | data formatting | bytes 33554432 | tf_op jit(solution)/shard_map/reshape | solution.py:121
  249.1 17.8 %copy.63 = f32[256,128,128]{0,2,1:T(8,128)} copy(f32[256,128,128]{2,1,0:T(8,128)} %convolution_select_fusion.1) | data formatting | bytes 33554432 | tf_op jit(solution)/shard_map/reshape | solution.py:118
  266.9 18.0 %pad_add_fusion = f32[256,16512]{0,1:T(8,128)} fusion(f32[256,16384]{0,1:T(8,128)} %bitcast.63, f32[256,16384]{0,1:T(8,128)} %bitcast.64), kind=kLoop, calls=%fused_computation | loop fusion | flops 4227072 | bytes 50462720 | tf_op jit(solution)/shard_map/add | solution.py:123
  284.9 18.0 %reshape.93 = f32[256,128,129]{0,2,1:T(8,128)} reshape(f32[256,16512]{0,1:T(8,128)} %pad_add_fusion) | data formatting | bytes 33816576 | tf_op jit(solution)/shard_map/reshape | solution.py:123
  302.9 7.3 %reduce_sum.18 = bf16[256,129]{0,1:T(8,128)(2,1)S(1)} reduce(f32[256,128,129]{0,2,1:T(8,128)} %reshape.93, f32[]{:T(128)} %constant.128.clone.1), dimensions={1}, to_apply=%region_0.1 | reduce | flops 4194048 | bytes 16974340 | tf_op jit(solution)/shard_map/reduce_sum | solution.py:123
  311.2 10.3 %fusion = f32[256,16,128]{2,1,0:T(8,128)} fusion(pred[128,128]{1,0:T(8,128)(4,1)S(1)} %iota_compare_fusion, bf16[256,128,255]{2,1,0:T(8,128)(2,1)} %reshape.85, bf16[256,16,1,128]{3,2,1,0:T(2,128)(2,1)S(1)} %copy-done.1), kind=kOutput, calls=%fused_computation.5 | convolution fusion | flops 138412032 | bytes 11550720 | tf_op jit(solution)/shard_map/gki,gcbk->gcbi/dot_general | solution.py:105
  321.5 80.0 %all-reduce.4.cloned.1.call-done = bf16[256,128]{1,0:T(8,128)(2,1)} async-done(((bf16[256,128]{1,0:T(8,128)(2,1)}), bf16[256,128]{1,0:T(8,128)(2,1)}) %all-reduce.4.cloned.1.call-update) | async-done | bytes 65552 | tf_op jit(solution)/shard_map/psum | solution.py:125
  406.2 10.4 %add_convert_fusion = bf16[256,16,128]{2,1,0:T(8,128)(2,1)S(1)} fusion(f32[256,16,128]{2,1,0:T(8,128)} %fusion, pred[128,128]{1,0:T(8,128)(4,1)S(1)} %iota_compare_fusion, bf16[256,128,255]{2,1,0:T(8,128)(2,1)} %reshape.85, bf16[256,16,1,128]{3,2,1,0:T(2,128)(2,1)} %get-tuple-element.8), kind=kOutput, calls=%fused_computation.19 | convolution fusion | flops 139460608 | bytes 13647872 | tf_op jit(solution)/shard_map/gki,gcbk->gcbi/dot_general | solution.py:108
  (82 shorter events, 23.9 us)
Async XLA Ops:
  7.2 394.4 %all-reduce.4.cloned.1.call-start = ((), (), s32[]{:S(2)}) async-start(), calls=%async_computation | async-start | bytes 131072 | tf_op jit(solution)/shard_map/psum | solution.py:125
  7.9 4.9 %collective-permute-start.1 = (bf16[16,128]{1,0:T(8,128)(2,1)S(1)}, bf16[16,128]{1,0:T(8,128)(2,1)S(1)}, u32[]{:S(2)}, u32[]{:S(2)}) collective-permute-start(bf16[16,128]{1,0:T(8,128)(2,1)S(1)} %get-tuple-element.7), channel_id=1, source_target_pairs={{0,1},{1,2},{2,3},{3,4},{4,5},{5,6},{6,7},{7,8},{8,9},{9,10},{10,1... | collective-permute-start | bytes 12296 | tf_op jit(solution)/shard_map/ppermute | solution.py:69
  7.9 5.6 %collective-permute-start.2 = (bf16[16,128]{1,0:T(8,128)(2,1)S(1)}, bf16[16,128]{1,0:T(8,128)(2,1)S(1)}, u32[]{:S(2)}, u32[]{:S(2)}) collective-permute-start(bf16[16,128]{1,0:T(8,128)(2,1)S(1)} %get-tuple-element.7), channel_id=1, source_target_pairs={{0,15},{1,0},{2,1},{3,2},{4,3},{5,4},{6,5},{7,6},{8,7},{9,8},{10,9... | collective-permute-start | bytes 12296 | tf_op jit(solution)/shard_map/ppermute | solution.py:74
  10.6 147.8 %collective-permute-start = (bf16[128,4096]{1,0:T(8,128)(2,1)}, bf16[128,4096]{1,0:T(8,128)(2,1)}, u32[]{:S(2)}, u32[]{:S(2)}) collective-permute-start(bf16[128,4096]{1,0:T(8,128)(2,1)} %bitcast.70), channel_id=1, source_target_pairs={{0,1},{1,2},{2,3},{3,4},{4,5},{5,6},{6,7},{7,8},{8,9},{9,10},{10,1... | collective-permute-start | bytes 3145736 | tf_op jit(solution)/shard_map/ppermute | solution.py:23
  12.8 15.1 %collective-permute-start.3 = (bf16[16,128]{1,0:T(8,128)(2,1)S(1)}, bf16[16,128]{1,0:T(8,128)(2,1)S(1)}, u32[]{:S(2)}, u32[]{:S(2)}) collective-permute-start(bf16[16,128]{1,0:T(8,128)(2,1)S(1)} %collective-permute-done.1), channel_id=1, source_target_pairs={{0,1},{1,2},{2,3},{3,4},{4,5},{5,6},{6,7},{7,8},{8,9},{9,10},{10,1... | collective-permute-start | bytes 12296 | tf_op jit(solution)/shard_map/ppermute | solution.py:69
  13.6 14.4 %collective-permute-start.4 = (bf16[16,128]{1,0:T(8,128)(2,1)S(1)}, bf16[16,128]{1,0:T(8,128)(2,1)S(1)}, u32[]{:S(2)}, u32[]{:S(2)}) collective-permute-start(bf16[16,128]{1,0:T(8,128)(2,1)S(1)} %collective-permute-done.2), channel_id=1, source_target_pairs={{0,15},{1,0},{2,1},{3,2},{4,3},{5,4},{6,5},{7,6},{8,7},{9,8},{10,9... | collective-permute-start | bytes 12296 | tf_op jit(solution)/shard_map/ppermute | solution.py:74
  28.0 3.9 collective-permute-start.5
  28.0 4.0 collective-permute-start.6
  31.9 3.9 collective-permute-start.7
  31.9 3.9 collective-permute-start.8
  35.8 3.9 collective-permute-start.9
  35.9 3.9 collective-permute-start.10
  39.8 3.9 collective-permute-start.11
  39.8 3.9 collective-permute-start.12
  43.7 3.9 collective-permute-start.13
  43.7 3.9 collective-permute-start.14
  47.6 3.9 collective-permute-start.15
  101.5 56.8 %copy-start.6 = (bf16[1,128,4096]{2,1,0:T(8,128)(2,1)S(1)}, bf16[1,128,4096]{2,1,0:T(8,128)(2,1)}, u32[]{:S(2)}) copy-start(bf16[1,128,4096]{2,1,0:T(8,128)(2,1)} %param.7) | copy-start | bytes 3145732
  167.8 9.7 %copy-start.2 = (bf16[256,16,1,128]{3,2,1,0:T(2,128)(2,1)}, bf16[256,16,1,128]{3,2,1,0:T(2,128)(2,1)S(1)}, u32[]{:S(2)}) copy-start(bf16[256,16,1,128]{3,2,1,0:T(2,128)(2,1)S(1)} %get-tuple-element.11) | copy-start | bytes 3145732
  167.8 9.7 %copy-start.4 = (bf16[256,16,1,128]{3,2,1,0:T(2,128)(2,1)}, bf16[256,16,1,128]{3,2,1,0:T(2,128)(2,1)S(1)}, u32[]{:S(2)}) copy-start(bf16[256,16,1,128]{3,2,1,0:T(2,128)(2,1)S(1)} %get-tuple-element.10) | copy-start | bytes 3145732
  189.1 2.2 copy-start.7
  193.9 14.2 %collective-permute-start.16 = (bf16[128,4096]{1,0:T(8,128)(2,1)S(1)}, bf16[128,4096]{1,0:T(8,128)(2,1)S(1)}, u32[]{:S(2)}, u32[]{:S(2)}) collective-permute-start(bf16[128,4096]{1,0:T(8,128)(2,1)S(1)} %get-tuple-element.12), channel_id=1, source_target_pairs={{1,0},{2,1},{3,2},{4,3},{5,4},{6,5},{7,6},{8,7},{9,8},{10,9},{11,1... | collective-permute-start | bytes 3145736 | tf_op jit(solution)/shard_map/ppermute | solution.py:23
  213.3 3.8 copy-start.5
  217.1 7.2 %copy-start = (bf16[256,16,1,128]{3,2,1,0:T(2,128)(2,1)}, bf16[256,16,1,128]{3,2,1,0:T(2,128)(2,1)S(1)}, u32[]{:S(2)}) copy-start(bf16[256,16,1,128]{3,2,1,0:T(2,128)(2,1)S(1)} %get-tuple-element.9) | copy-start | bytes 3145732
  217.1 7.2 %copy-start.3 = (bf16[256,16,1,128]{3,2,1,0:T(2,128)(2,1)S(1)}, bf16[256,16,1,128]{3,2,1,0:T(2,128)(2,1)}, u32[]{:S(2)}) copy-start(bf16[256,16,1,128]{3,2,1,0:T(2,128)(2,1)} %copy-done.2) | copy-start | bytes 3145732
  302.9 8.3 %copy-start.1 = (bf16[256,16,1,128]{3,2,1,0:T(2,128)(2,1)S(1)}, bf16[256,16,1,128]{3,2,1,0:T(2,128)(2,1)}, u32[]{:S(2)}) copy-start(bf16[256,16,1,128]{3,2,1,0:T(2,128)(2,1)} %copy-done) | copy-start | bytes 3145732
  311.2 93.5 %copy-start.8 = (f32[1,16,128]{2,1,0:T(8,128)S(1)}, f32[1,16,128]{2,1,0:T(8,128)}, u32[]{:S(2)}) copy-start(f32[1,16,128]{2,1,0:T(8,128)} %param.10) | copy-start | bytes 24580
  311.2 93.5 %copy-start.9 = (f32[1,16,128]{2,1,0:T(8,128)S(1)}, f32[1,16,128]{2,1,0:T(8,128)}, u32[]{:S(2)}) copy-start(f32[1,16,128]{2,1,0:T(8,128)} %param.12) | copy-start | bytes 24580
  311.2 93.5 %copy-start.10 = (f32[1,16,128]{2,1,0:T(8,128)S(1)}, f32[1,16,128]{2,1,0:T(8,128)}, u32[]{:S(2)}) copy-start(f32[1,16,128]{2,1,0:T(8,128)} %param.11) | copy-start | bytes 24580
  404.7 13.2 %collective-permute-start.17 = (f32[16,128]{1,0:T(8,128)S(1)}, f32[16,128]{1,0:T(8,128)S(1)}, u32[]{:S(2)}, u32[]{:S(2)}) collective-permute-start(f32[16,128]{1,0:T(8,128)S(1)} %fusion.17), channel_id=1, source_target_pairs={{0,16},{16,0},{1,17},{17,1},{2,18},{18,2},{3,19},{19,3},{4,20},{20... | collective-permute-start | bytes 24584 | tf_op jit(solution)/shard_map/ppermute | solution.py:17
Sparse Core Ops, SparseCore 0:
  311.3 90.2 all-reduce.3
